TPU v7x, 32 devices: a whole 2x2x4 slice. The times are simulated.
32 devices in a mesh: seq: 8 (over z, core), tp: 4 (over y, x).
Axes of the slice: x: 2, y: 2, z: 4, core: 2. Of those that a mesh axis runs over, the one named last changes fastest.
Arguments:
- qkv: bfloat16 [3, 4, 128, 3072], P(None, None, ('seq', 'tp')), may hold values from -6 to 6
- positions: int32 [3, 4, 128], P(None, None, ('seq', 'tp')), may hold values from 0 to 31, as said below
- w_proj: bfloat16 [3072, 64], replicated, may hold values from -0.21875 to 0.21875
- latents: bfloat16 [4, 128, 64], P(None, 'seq'), may hold values from -6 to 6
- embed_w: bfloat16 [64, 2048], replicated, may hold values from -0.75 to 0.75
- up_w: bfloat16 [2048, 8192], P(None, 'tp'), may hold values from -0.125 to 0.125
- down_w: bfloat16 [8192, 2048], P('tp'), may hold values from -0.0625 to 0.0625
- head_w: bfloat16 [2048, 1000], P(('seq', 'tp')), may hold values from -3 to 3
- labels: int32 [4], replicated, may hold values from 0 to 999
- timesteps: int32 [4], replicated, may hold values from 0 to 999
Outputs:
- guided: bfloat16 [4, 128, 64], P(None, ('seq', 'tp'))
Inputs may be any that keep to these rules, and one draw needn't show every extreme that they name: For each video the tokens are the cells of a stack of frames of 32 x 32 cells, each cell once, in shuffled order; positions[0] is the frame, positions[1] the row, positions[2] the column.
All inputs are finite; a program needn't handle non-finite values.
Results may differ from a plain program's by a relative error of at most 0.0095.
Values may be sent and summed in bfloat16 or wider, within the bound.
No kernel may reach another device: no remote copies, remote signals or barrier semaphores. Data moves between devices by JAX's collectives and lax.ppermute only.
A program may use at most 64 MiB of HBM per device.

v0:
```python
import jax
import jax.numpy as jnp
from jax import lax
from jax.sharding import PartitionSpec as P

HEADS = 24
HEAD_DIM = 128
GUIDANCE = 0.1


def rope_angles(positions, head_dim):
    frame_width = head_dim // 8
    plane_width = (head_dim - frame_width) // 2
    pieces = []
    for axis, width in zip(range(3), (frame_width, plane_width, plane_width)):
        freqs = 10000.0 ** (-jnp.arange(0, width, 2, dtype=jnp.float32) / width)
        pieces.append(positions[axis][..., None] * freqs)
    return jnp.concatenate(pieces, axis=-1)


def rotate(values, angles):
    half = values.shape[-1] // 2
    floats = values.astype(jnp.float32)
    first = floats[..., :half]
    second = floats[..., half:]
    cosine = jnp.cos(angles)[:, :, None, :]
    sine = jnp.sin(angles)[:, :, None, :]
    turned = jnp.concatenate(
        [first * cosine - second * sine, first * sine + second * cosine], axis=-1
    )
    return turned.astype(jnp.bfloat16)


def gelu_slope(values):
    cdf = 0.5 * (1.0 + jax.scipy.special.erf(values * 0.7071067811865476))
    pdf = jnp.exp(-0.5 * values * values) * 0.3989422804014327
    return cdf + values * pdf


def pairs_first(array):
    samples, tokens = (array.shape[0], array.shape[1])
    return array.transpose(0, 2, 1, 3).reshape(samples * HEADS, tokens, HEAD_DIM)


def per_device(qkv, positions, w_proj, latents, embed_w, up_w, down_w, head_w, labels, timesteps):
    samples, tok_dev = (qkv.shape[1], qkv.shape[2])
    angles = rope_angles(positions.astype(jnp.float32), HEAD_DIM)
    shaped = (samples, tok_dev, HEADS, HEAD_DIM)
    queries = rotate(qkv[0].reshape(shaped), angles)
    keys_tok = rotate(qkv[1].reshape(shaped), angles)
    values_tok = qkv[2].reshape(shaped)
    moved = lax.all_to_all(
        jnp.stack([pairs_first(queries), pairs_first(keys_tok), pairs_first(values_tok)]),
        "seq",
        split_axis=1,
        concat_axis=2,
        tiled=True,
    )
    query_pairs = moved[0]
    pair_count, query_count = (query_pairs.shape[0], query_pairs.shape[1])
    running = jnp.full((pair_count, query_count), -jnp.inf, jnp.float32)
    total = jnp.zeros((pair_count, query_count), jnp.float32)
    accum = jnp.zeros((pair_count, query_count, HEAD_DIM), jnp.float32)
    key_piece = lax.all_gather(moved[1], "tp", axis=1, tiled=True)
    value_piece = lax.all_gather(moved[2], "tp", axis=1, tiled=True)
    scores = jnp.einsum(
        "iqd,ikd->iqk", query_pairs, key_piece, preferred_element_type=jnp.float32
    ) * HEAD_DIM ** (-0.5)
    newest = jnp.max(scores, axis=-1)
    factor = jnp.exp(running - newest)
    weights = jnp.exp(scores - newest[..., None])
    total = total * factor + jnp.sum(weights, axis=-1)
    accum = accum * factor[..., None] + jnp.einsum(
        "iqk,ikd->iqd",
        weights.astype(jnp.bfloat16),
        value_piece,
        preferred_element_type=jnp.float32,
    )
    running, total, accum = (newest, total, accum)
    attended = (accum / total[..., None]).astype(jnp.bfloat16)
    returned = lax.all_to_all(attended, "seq", split_axis=1, concat_axis=0, tiled=True)
    returned = returned.reshape(samples, HEADS, tok_dev, HEAD_DIM).transpose(0, 2, 1, 3)
    returned = returned.reshape(samples, tok_dev, HEADS * HEAD_DIM)
    eps = jnp.dot(returned, w_proj, preferred_element_type=jnp.float32)
    seq_len = latents.shape[1] * lax.axis_size("seq")
    tp_index = lax.axis_index("tp")
    emb = jnp.dot(latents, embed_w, preferred_element_type=jnp.float32).astype(jnp.bfloat16)
    hidden = jnp.dot(emb, up_w, preferred_element_type=jnp.float32)
    act = jax.nn.gelu(hidden, approximate=False).astype(jnp.bfloat16)
    branch = jnp.dot(act, down_w, preferred_element_type=jnp.float32)
    own_emb = lax.dynamic_slice_in_dim(emb, tp_index * tok_dev, tok_dev, 1).astype(jnp.float32)
    partial_pool = jnp.sum(branch, axis=1) + jnp.sum(own_emb, axis=1)
    head_rows = head_w.shape[0]
    flat_index = lax.axis_index("seq") * lax.axis_size("tp") + tp_index
    pooled = lax.psum(partial_pool, ("seq", "tp")) / seq_len
    pooled_share = lax.dynamic_slice_in_dim(pooled, flat_index * head_rows, head_rows, 1)
    head_float = head_w.astype(jnp.float32)
    logit_terms = jnp.dot(pooled_share, head_float, precision=lax.Precision.HIGHEST)
    logits = lax.psum(logit_terms, ("seq", "tp"))
    probs = jax.nn.softmax(logits, axis=-1)
    onehot = (labels[:, None] == jnp.arange(logits.shape[1], dtype=jnp.int32)[None, :]).astype(
        jnp.float32
    )
    grad_share = jnp.dot(onehot - probs, head_float.T, precision=lax.Precision.HIGHEST)
    dpool = lax.all_gather(grad_share, ("seq", "tp"), axis=1, tiled=True)
    dact = jnp.dot(dpool, down_w.astype(jnp.float32).T, precision=lax.Precision.HIGHEST)
    dh1 = (gelu_slope(hidden) * dact[:, None, :]).astype(jnp.bfloat16)
    demb = jnp.einsum("btf,cf->btc", dh1, up_w, preferred_element_type=jnp.float32)
    embed_float = embed_w.astype(jnp.float32)
    dx_terms = jnp.einsum("btc,lc->btl", demb, embed_float, precision=lax.Precision.HIGHEST)
    dx_mine = lax.psum_scatter(
        dx_terms.astype(jnp.bfloat16), "tp", scatter_dimension=1, tiled=True
    ).astype(jnp.float32)
    dx_pool = jnp.dot(dpool, embed_float.T, precision=lax.Precision.HIGHEST)
    dx_total = dx_mine + dx_pool[:, None, :]
    phase = (timesteps.astype(jnp.float32) / 1000.0 + 0.008) / 1.008 * (jnp.pi / 2)
    abar = jnp.cos(phase) ** 2
    scale = GUIDANCE * jnp.sqrt(1.0 - abar)
    return (eps - scale[:, None, None] * dx_total).astype(jnp.bfloat16)


def solution(mesh):
    placed = (
        P(None, None, ("seq", "tp"), None),
        P(None, None, ("seq", "tp")),
        P(),
        P(None, "seq", None),
        P(),
        P(None, "tp"),
        P("tp", None),
        P(("seq", "tp"), None),
        P(),
        P(),
    )
    return jax.shard_map(
        per_device,
        mesh=mesh,
        in_specs=placed,
        out_specs=P(None, ("seq", "tp"), None),
        check_vma=False,
    )
```

profile of v0, /device:TPU:0, one launch (start us, length us, event | category | flops | bytes accessed | tf_op | source)
XLA Modules:
  0.0 233.0 jit_solution(14291918177690481106)
XLA Ops:
  0.0 1.1 slice_convert_fusion.1
  1.2 0.1 reshape.93
  1.3 0.1 fusion.126
  1.4 0.7 convert_element_type.55
  2.1 0.1 copy.25
  2.2 0.1 copy.26
  2.3 0.1 copy.24
  2.4 0.1 reshape.94
  2.5 0.1 fusion.127
  2.6 0.1 broadcast_multiply_fusion.2
  2.7 0.1 broadcast_multiply_fusion.1
  2.7 0.2 fusion.124
  2.9 0.1 subtract_convert_fusion.1
  3.0 0.1 pad_maximum_fusion.1
  3.2 0.9 copy.29
  4.1 6.4 %all-to-all-start = ((bf16[3,96,4,128]{3,2,0,1:T(4,128)(2,1)}), bf16[3,96,4,128]{3,2,0,1:T(4,128)(2,1)S(1)}, u32[]{:S(2)}, u32[]{:S(2)}) async-start(bf16[3,96,4,128]{3,2,0,1:T(4,128)(2,1)} %copy.29), calls=%async_computation | async-start | bytes 589824 | tf_op jit(solution)/shard_map/all_to_all | solution.py:52
  10.4 1.2 convolution_convert_fusion
  11.6 5.1 %fusion.72 = (u8[16,2048]{1,0:T(8,128)(4,1)S(1)}, u8[16,2048]{1,0:T(8,128)(4,1)S(1)}, f32[4,16,2048]{2,1,0:T(8,128)S(1)}) fusion(bf16[4,16,2048]{2,1,0:T(8,128)(2,1)S(1)} %convolution_convert_fusion, bf16[2048,2048]{1,0:T(8,128)(2,1)} %param.15), kind=kOutput, calls=%fused_computation.95 | convolution fusion | flops 538509312 | bytes 9240576 | tf_op jit(solution)/shard_map/dot_general | solution.py:88
  16.7 0.1 convert_reduce_fusion
  16.8 0.0 copy-start.2
  16.8 6.0 %fusion.6 = f32[4,2048]{1,0:T(4,128)S(1)} fusion(bf16[2048,2048]{1,0:T(8,128)(2,1)} %param.16, f32[4,16,2048]{2,1,0:T(8,128)S(1)} %get-tuple-element.34, u8[16,2048]{1,0:T(8,128)(4,1)S(1)} %get-tuple-element.6, u8[16,2048]{1,0:T(8,128)(4,1)S(1)} %get-tuple-element.5), kind=kOutput, calls=%fused_computation.7 | convolution fusion | flops 546168832 | bytes 9011200 | tf_op jit(solution)/shard_map/dot_general | solution.py:90
  22.8 40.9 %psum.14 = f32[4,2048]{1,0:T(4,128)S(1)} all-reduce(f32[4,2048]{1,0:T(4,128)S(1)} %add.59), channel_id=1, replica_groups=mesh['seq'=8,'tp'=4] {'seq','tp'}, use_global_device_ids=true, to_apply=%region_4.0 | all-reduce | flops 8192 | bytes 65536 | tf_op jit(solution)/shard_map/psum | solution.py:95
  63.8 0.2 fusion.82
  64.0 40.0 %psum.15 = f32[4,1000]{1,0:T(4,128)S(1)} all-reduce(f32[4,1000]{1,0:T(4,128)S(1)} %fusion.82), channel_id=1, replica_groups=mesh['seq'=8,'tp'=4] {'seq','tp'}, use_global_device_ids=true, to_apply=%region_5.0 | all-reduce | flops 4000 | bytes 32000 | tf_op jit(solution)/shard_map/psum | solution.py:99
  104.0 0.1 reduce_max.19
  104.2 0.2 fusion.78
  104.4 0.2 convolution_bitcast_fusion
  104.6 66.3 %all-gather = f32[32,64,4]{1,2,0:T(4,128)S(1)} all-gather(f32[1,64,4]{1,2,0:T(4,128)S(1)} %convolution_bitcast_fusion), channel_id=1, replica_groups=mesh['seq'=8,'tp'=4] {'seq','tp'}, dimensions={0}, use_global_device_ids=true | all-gather | bytes 33792 | tf_op jit(solution)/shard_map/all_gather | solution.py:105
  170.9 0.1 reshape.88
  171.0 8.9 %fusion.129 = f32[4,2048]{1,0:T(4,128)S(1)} fusion(f32[2048,4]{0,1:T(4,128)S(1)} %reshape.88, bf16[2048,2048]{1,0:T(8,128)(2,1)} %param.16), kind=kOutput, calls=%fused_computation.170 | convolution fusion | flops 201326592 | bytes 8454144 | tf_op jit(solution)/shard_map/dot_general | solution.py:106
  179.9 0.0 copy-start.1
  179.9 6.1 %fusion.2 = f32[4,16,2048]{2,1,0:T(8,128)S(1)} fusion(bf16[2048,2048]{1,0:T(8,128)(2,1)} %param.15, f32[4,16,2048]{2,1,0:T(8,128)S(1)} %get-tuple-element.34, f32[4,2048]{1,0:T(4,128)S(1)} %fusion.129), kind=kOutput, calls=%fused_computation.2 | convolution fusion | flops 538181632 | bytes 9469952 | tf_op jit(solution)/shard_map/btf,cf->btc/dot_general | solution.py:108
  186.0 0.6 dynamic-slice
  187.3 0.4 convolution_convert_fusion.1
  187.7 13.9 %all-reduce = bf16[4,16,64]{2,1,0:T(8,128)(2,1)S(1)} all-reduce(bf16[4,16,64]{2,1,0:T(8,128)(2,1)S(1)} %convolution_convert_fusion.1), channel_id=2, replica_groups=mesh['seq'=8,'tp'=4] {'tp'}, use_global_device_ids=true, to_apply=%region_8.0.clone | all-reduce | flops 4096 | bytes 16384
  201.5 0.3 fusion.130
  201.8 0.1 copy.30
  201.9 0.1 fusion.125
  202.1 8.9 %all_gather.10 = bf16[12,128,128]{2,1,0:T(8,128)(2,1)S(1)} all-gather(bf16[12,32,128]{2,1,0:T(8,128)(2,1)S(1)} %bitcast.77), channel_id=1, replica_groups=mesh['seq'=8,'tp'=4] {'tp'}, dimensions={1}, use_global_device_ids=true | all-gather | bytes 491520 | tf_op jit(solution)/shard_map/all_gather | solution.py:65
  211.1 9.3 %all_gather.9 = bf16[12,128,128]{2,1,0:T(8,128)(2,1)S(1)} all-gather(bf16[12,32,128]{2,1,0:T(8,128)(2,1)S(1)} %bitcast.78), channel_id=1, replica_groups=mesh['seq'=8,'tp'=4] {'tp'}, dimensions={1}, use_global_device_ids=true | all-gather | bytes 491520 | tf_op jit(solution)/shard_map/all_gather | solution.py:64
  220.4 0.4 fusion.128
  220.8 0.2 fusion.69
  221.1 0.3 fusion.10
  221.4 0.7 copy.34
  222.1 3.4 %all-to-all-start.1 = ((bf16[12,32,128]{2,0,1:T(8,128)(2,1)}), bf16[12,32,128]{2,0,1:T(8,128)(2,1)S(1)}, u32[]{:S(2)}, u32[]{:S(2)}) async-start(bf16[12,32,128]{2,0,1:T(8,128)(2,1)} %copy.34), calls=%async_computation.1 | async-start | bytes 262144 | tf_op jit(solution)/shard_map/all_to_all | solution.py:81
  225.5 0.1 sqrt_multiply_fusion
  225.5 6.6 %all-to-all-done.1 = bf16[12,32,128]{2,0,1:T(8,128)(2,1)S(1)} async-done(((bf16[12,32,128]{2,0,1:T(8,128)(2,1)}), bf16[12,32,128]{2,0,1:T(8,128)(2,1)S(1)}, u32[]{:S(2)}, u32[]{:S(2)}) %all-to-all-start.1) | async-done | bytes 98336 | tf_op jit(solution)/shard_map/all_to_all | solution.py:81
  232.2 0.8 fusion.11
  (24 shorter events, 0.3 us)
Async XLA Ops:
  0.0 232.2 %copy-start = (bf16[3072,64]{0,1:T(8,128)(2,1)S(1)}, bf16[3072,64]{0,1:T(8,128)(2,1)}, u32[]{:S(2)}) copy-start(bf16[3072,64]{0,1:T(8,128)(2,1)} %param.12) | copy-start | bytes 1179652
  4.1 197.8 %all-to-all-start = ((bf16[3,96,4,128]{3,2,0,1:T(4,128)(2,1)}), bf16[3,96,4,128]{3,2,0,1:T(4,128)(2,1)S(1)}, u32[]{:S(2)}, u32[]{:S(2)}) async-start(bf16[3,96,4,128]{3,2,0,1:T(4,128)(2,1)} %copy.29), calls=%async_computation | async-start | bytes 589824 | tf_op jit(solution)/shard_map/all_to_all | solution.py:52
  16.8 47.0 %copy-start.2 = (bf16[64,1000]{1,0:T(8,128)(2,1)S(1)}, bf16[64,1000]{1,0:T(8,128)(2,1)}, u32[]{:S(2)}) copy-start(bf16[64,1000]{1,0:T(8,128)(2,1)} %param.17) | copy-start | bytes 384004
  16.8 87.6 %copy-start.3 = (s32[4]{0:T(128)S(1)}, s32[4]{0:T(128)}, u32[]{:S(2)}) copy-start(s32[4]{0:T(128)} %param.18) | copy-start | bytes 52
  179.9 6.1 %copy-start.5 = (u32[32]{0:T(128)S(1)}, u32[32]{0:T(128)}, u32[]{:S(2)}) copy-start(u32[32]{0:T(128)} %constant.123) | copy-start | bytes 388
  179.9 7.4 %copy-start.1 = (bf16[64,2048]{1,0:T(8,128)(2,1)S(1)}, bf16[64,2048]{1,0:T(8,128)(2,1)}, u32[]{:S(2)}) copy-start(bf16[64,2048]{1,0:T(8,128)(2,1)} %param.14) | copy-start | bytes 786436
  179.9 45.5 %copy-start.4 = (s32[4]{0:T(128)S(1)}, s32[4]{0:T(128)}, u32[]{:S(2)}) copy-start(s32[4]{0:T(128)} %param.19) | copy-start | bytes 52
  222.1 10.1 %all-to-all-start.1 = ((bf16[12,32,128]{2,0,1:T(8,128)(2,1)}), bf16[12,32,128]{2,0,1:T(8,128)(2,1)S(1)}, u32[]{:S(2)}, u32[]{:S(2)}) async-start(bf16[12,32,128]{2,0,1:T(8,128)(2,1)} %copy.34), calls=%async_computation.1 | async-start | bytes 262144 | tf_op jit(solution)/shard_map/all_to_all | solution.py:81
where the time goes:
time: 234 us; the launch traced here: 233 us
  blocking collectives  179 us (76%)
  matrix products  29.8 us (13%)
  starting transfers between devices  9.72 us (4%)
  waiting for transfers between devices  6.62 us (3%)
  local copies, waits for them, and re-layouts  3.35 us (1%)
  other arithmetic  3.16 us (1%)
    all_gather x1, blocking collectives, per_device(): dpool = lax.all_gather(grad_share, ('seq', 'tp'), axis=1, tiled=True)  66.3 us
    psum x1, blocking collectives, per_device(): pooled = lax.psum(partial_pool, ('seq', 'tp')) / seq_len  40.9 us
    psum x1, blocking collectives, per_device(): logits = lax.psum(logit_terms, ('seq', 'tp'))  40 us
    unnamed x1, blocking collectives  13.9 us
    all_gather x1, blocking collectives, per_device(): key_piece = lax.all_gather(moved[1], 'tp', axis=1, tiled=True)  9.33 us
    all_gather x1, blocking collectives, per_device(): value_piece = lax.all_gather(moved[2], 'tp', axis=1, tiled=True)  8.92 us
    dot_general x1, matrix products, per_device(): jnp.dot(dpool, down_w.astype(jnp.float32).T, precision=lax.Precision.HIGH...  8.9 us
    all_to_all x1, waiting for transfers between devices, per_device(): lax.all_to_all(attended, 'seq', split_axis=1, concat_axis=0, tiled=True)  6.62 us
  transfers between devices with their start and end apart: 2, of which 1 were waited for; matrix products, arithmetic and copies ran while one was open for 13% of the time, Pallas kernels for 0%

commit v1 on v0

--- a/solution.py
+++ b/solution.py
@@ -102,7 +102,15 @@
         jnp.float32
     )
     grad_share = jnp.dot(onehot - probs, head_float.T, precision=lax.Precision.HIGHEST)
-    dpool = lax.all_gather(grad_share, ("seq", "tp"), axis=1, tiled=True)
+    ways, here = (lax.axis_size(("seq", "tp")), lax.axis_index(("seq", "tp")))
+    grown, reach = (grad_share, 1)
+    while reach < ways:
+        theirs = lax.ppermute(grown, ("seq", "tp"), [(d, d ^ reach) for d in range(ways)])
+        mine_first = jnp.concatenate([grown, theirs], axis=1)
+        theirs_first = jnp.concatenate([theirs, grown], axis=1)
+        grown = jnp.where(here & reach == 0, mine_first, theirs_first)
+        reach = 2 * reach
+    dpool = grown
     dact = jnp.dot(dpool, down_w.astype(jnp.float32).T, precision=lax.Precision.HIGHEST)
     dh1 = (gelu_slope(hidden) * dact[:, None, :]).astype(jnp.bfloat16)
     demb = jnp.einsum("btf,cf->btc", dh1, up_w, preferred_element_type=jnp.float32)

time: 234 us -> 185 us (0.79)
  blocking collectives: 179 us -> 118 us
  waiting for transfers between devices: 6.62 us -> 16 us
  starting transfers between devices: 9.72 us -> 14.8 us
    all_gather x1 -> x0, blocking collectives: 66.3 us -> none  [per_device(): dpool = lax.all_gather(grad_share, ('seq', 'tp'), axis=1, tiled=True)]
    ppermute x0 -> x5, waiting for transfers between devices: none -> 9.64 us  [per_device(): lax.ppermute(grown, ('seq', 'tp'), [(d, d ^ reach) for d in range(ways)])]
    ppermute x0 -> x5, starting transfers between devices: none -> 7.85 us  [per_device(): lax.ppermute(grown, ('seq', 'tp'), [(d, d ^ reach) for d in range(ways)])]
    all_to_all x1, starting transfers between devices: 6.35 us -> 3.56 us  [per_device(): lax.all_to_all(jnp.stack([pairs_first(queries), pairs_first(keys_tok), pa...]
    unnamed x1, blocking collectives: 13.9 us -> 16.6 us
  transfers between devices with their start and end apart: 2 -> 7, of which waited for: 1 -> 5; matrix products, arithmetic and copies ran while one was open for 13% -> 10% of each run, Pallas kernels for 0% -> 0%
where the time goes in v1:
time: 185 us; the launch traced here: 184 us
  blocking collectives  118 us (64%)
  matrix products  29.9 us (16%)
  waiting for transfers between devices  16 us (9%)
  starting transfers between devices  14.8 us (8%)
  local copies, waits for them, and re-layouts  3.25 us (2%)
    psum x1, blocking collectives, per_device(): pooled = lax.psum(partial_pool, ('seq', 'tp')) / seq_len  42.1 us
    psum x1, blocking collectives, per_device(): logits = lax.psum(logit_terms, ('seq', 'tp'))  40.2 us
    unnamed x1, blocking collectives  16.6 us
    all_gather x1, blocking collectives, per_device(): key_piece = lax.all_gather(moved[1], 'tp', axis=1, tiled=True)  10.1 us
    ppermute x5, waiting for transfers between devices, per_device(): lax.ppermute(grown, ('seq', 'tp'), [(d, d ^ reach) for d in range(ways)])  9.64 us
    dot_general x1, matrix products, per_device(): jnp.dot(dpool, down_w.astype(jnp.float32).T, precision=lax.Precision.HIGH...  8.9 us
    all_gather x1, blocking collectives, per_device(): value_piece = lax.all_gather(moved[2], 'tp', axis=1, tiled=True)  8.62 us
    ppermute x5, starting transfers between devices, per_device(): lax.ppermute(grown, ('seq', 'tp'), [(d, d ^ reach) for d in range(ways)])  7.85 us
  transfers between devices with their start and end apart: 7, of which 5 were waited for; matrix products, arithmetic and copies ran while one was open for 10% of the time, Pallas kernels for 0%

profile of v1, /device:TPU:0, one launch (start us, length us, event | category | flops | bytes accessed | tf_op | source)
XLA Modules:
  0.0 184.1 jit_solution(11486707913923413022)
XLA Ops:
  0.0 1.2 convolution_convert_fusion
  1.2 5.1 %fusion.72 = (u8[16,2048]{1,0:T(8,128)(4,1)S(1)}, u8[16,2048]{1,0:T(8,128)(4,1)S(1)}, f32[4,16,2048]{2,1,0:T(8,128)S(1)}) fusion(bf16[4,16,2048]{2,1,0:T(8,128)(2,1)S(1)} %convolution_convert_fusion, bf16[2048,2048]{1,0:T(8,128)(2,1)} %param.15), kind=kOutput, calls=%fused_computation.94 | convolution fusion | flops 538509312 | bytes 9240576 | tf_op jit(solution)/shard_map/dot_general | solution.py:88
  6.3 0.1 convert_reduce_fusion
  6.5 6.0 %fusion.6 = f32[4,2048]{1,0:T(4,128)S(1)} fusion(bf16[2048,2048]{1,0:T(8,128)(2,1)} %param.16, f32[4,16,2048]{2,1,0:T(8,128)S(1)} %get-tuple-element.34, u8[16,2048]{1,0:T(8,128)(4,1)S(1)} %get-tuple-element.6, u8[16,2048]{1,0:T(8,128)(4,1)S(1)} %get-tuple-element.5), kind=kOutput, calls=%fused_computation.7 | convolution fusion | flops 546168832 | bytes 9011200 | tf_op jit(solution)/shard_map/dot_general | solution.py:90
  12.5 42.1 %psum.14 = f32[4,2048]{1,0:T(4,128)S(1)} all-reduce(f32[4,2048]{1,0:T(4,128)S(1)} %add.61), channel_id=1, replica_groups=mesh['seq'=8,'tp'=4] {'seq','tp'}, use_global_device_ids=true, to_apply=%region_4.0 | all-reduce | flops 8192 | bytes 65536 | tf_op jit(solution)/shard_map/psum | solution.py:95
  54.7 0.2 fusion.85
  54.9 40.2 %psum.15 = f32[4,1000]{1,0:T(4,128)S(1)} all-reduce(f32[4,1000]{1,0:T(4,128)S(1)} %fusion.85), channel_id=1, replica_groups=mesh['seq'=8,'tp'=4] {'seq','tp'}, use_global_device_ids=true, to_apply=%region_5.0 | all-reduce | flops 4000 | bytes 32000 | tf_op jit(solution)/shard_map/psum | solution.py:99
  95.1 0.1 reduce_max.19
  95.2 0.2 fusion.79
  95.4 0.2 fusion.77
  95.7 2.3 %collective-permute-start = (f32[4,64]{1,0:T(4,128)S(1)}, f32[4,64]{1,0:T(4,128)S(1)}, u32[]{:S(2)}, u32[]{:S(2)}) collective-permute-start(f32[4,64]{1,0:T(4,128)S(1)} %fusion.77), channel_id=1, source_target_pairs={{0,1},{1,0},{2,3},{3,2},{4,5},{5,4},{6,7},{7,6},{8,9},{9,8},{10,11... | collective-permute-start | bytes 3080 | tf_op jit(solution)/shard_map/ppermute | solution.py:108
  98.1 0.1 reshape.91
  98.2 0.1 fusion.131
  98.3 0.1 copy.24
  98.4 0.1 copy.25
  98.5 0.1 copy.23
  98.6 0.1 reshape.92
  98.7 0.1 fusion.132
  99.0 0.2 fusion.129
  99.1 0.4 collective-permute-done
  99.6 0.1 maximum_select_fusion.6
  99.6 2.0 %collective-permute-start.1 = (f32[4,128]{1,0:T(4,128)S(1)}, f32[4,128]{1,0:T(4,128)S(1)}, u32[]{:S(2)}, u32[]{:S(2)}) collective-permute-start(f32[4,128]{1,0:T(4,128)S(1)} %maximum_select_fusion.6), channel_id=1, source_target_pairs={{0,2},{1,3},{2,0},{3,1},{4,6},{5,7},{6,4},{7,5},{8,10},{9,11},{10,... | collective-permute-start | bytes 6152 | tf_op jit(solution)/shard_map/ppermute | solution.py:108
  101.7 0.1 subtract_convert_fusion.1
  101.8 1.4 collective-permute-done.1
  103.3 0.1 pad_maximum_fusion.1
  103.5 1.0 collective-permute-done.2
  104.4 0.5 collective-permute-start.3
  104.9 0.9 copy.28
  105.8 3.6 %all-to-all-start = ((bf16[3,96,4,128]{3,2,0,1:T(4,128)(2,1)}), bf16[3,96,4,128]{3,2,0,1:T(4,128)(2,1)S(1)}, u32[]{:S(2)}, u32[]{:S(2)}) async-start(bf16[3,96,4,128]{3,2,0,1:T(4,128)(2,1)} %copy.28), calls=%async_computation | async-start | bytes 589824 | tf_op jit(solution)/shard_map/all_to_all | solution.py:52
  109.4 3.0 %collective-permute-start.4 = (f32[4,1024]{1,0:T(4,128)S(1)}, f32[4,1024]{1,0:T(4,128)S(1)}, u32[]{:S(2)}, u32[]{:S(2)}) collective-permute-start(f32[4,1024]{1,0:T(4,128)S(1)} %maximum_select_fusion.1), channel_id=1, source_target_pairs={{0,16},{1,17},{2,18},{3,19},{4,20},{5,21},{6,22},{7,23},{8,24},{9,... | collective-permute-start | bytes 49160 | tf_op jit(solution)/shard_map/ppermute | solution.py:108
  112.4 0.6 dynamic-slice
  113.7 6.8 %collective-permute-done.4 = f32[4,1024]{1,0:T(4,128)S(1)} collective-permute-done((f32[4,1024]{1,0:T(4,128)S(1)}, f32[4,1024]{1,0:T(4,128)S(1)}, u32[]{:S(2)}, u32[]{:S(2)}) %collective-permute-start.4) | collective-permute-done | bytes 16416 | tf_op jit(solution)/shard_map/ppermute | solution.py:108
  120.5 8.9 %fusion.84 = f32[4,2048]{1,0:T(4,128)S(1)} fusion(bf16[2048,2048]{1,0:T(8,128)(2,1)} %param.16, f32[4,1024]{1,0:T(4,128)S(1)} %collective-permute-done.4, f32[4,1024]{1,0:T(4,128)S(1)} %maximum_select_fusion.1, pred[]{:T(512)S(6)} %eq.28), kind=kOutput, calls=%fused_computation.117 | convolution fusion | flops 201351168 | bytes 8454145 | tf_op jit(solution)/shard_map/dot_general | solution.py:114
  129.4 6.1 %fusion.2 = f32[4,16,2048]{2,1,0:T(8,128)S(1)} fusion(bf16[2048,2048]{1,0:T(8,128)(2,1)} %param.15, f32[4,16,2048]{2,1,0:T(8,128)S(1)} %get-tuple-element.34, f32[4,2048]{1,0:T(4,128)S(1)} %fusion.84), kind=kOutput, calls=%fused_computation.2 | convolution fusion | flops 538181632 | bytes 9469952 | tf_op jit(solution)/shard_map/btf,cf->btc/dot_general | solution.py:116
  135.5 0.4 convolution_convert_fusion.1
  135.9 16.6 %all-reduce = bf16[4,16,64]{2,1,0:T(8,128)(2,1)S(1)} all-reduce(bf16[4,16,64]{2,1,0:T(8,128)(2,1)S(1)} %convolution_convert_fusion.1), channel_id=2, replica_groups=mesh['seq'=8,'tp'=4] {'tp'}, use_global_device_ids=true, to_apply=%region_8.9.clone | all-reduce | flops 4096 | bytes 16384
  152.5 0.1 copy.29
  152.6 0.1 fusion.130
  152.7 8.6 %all_gather.7 = bf16[12,128,128]{2,1,0:T(8,128)(2,1)S(1)} all-gather(bf16[12,32,128]{2,1,0:T(8,128)(2,1)S(1)} %bitcast.69), channel_id=1, replica_groups=mesh['seq'=8,'tp'=4] {'tp'}, dimensions={1}, use_global_device_ids=true | all-gather | bytes 491520 | tf_op jit(solution)/shard_map/all_gather | solution.py:65
  161.4 10.1 %all_gather.6 = bf16[12,128,128]{2,1,0:T(8,128)(2,1)S(1)} all-gather(bf16[12,32,128]{2,1,0:T(8,128)(2,1)S(1)} %bitcast.70), channel_id=1, replica_groups=mesh['seq'=8,'tp'=4] {'tp'}, dimensions={1}, use_global_device_ids=true | all-gather | bytes 491520 | tf_op jit(solution)/shard_map/all_gather | solution.py:64
  171.5 0.4 fusion.133
  171.9 0.2 fusion.69
  172.2 0.3 fusion.10
  172.5 0.7 copy.33
  173.2 3.4 %all-to-all-start.1 = ((bf16[12,32,128]{2,0,1:T(8,128)(2,1)}), bf16[12,32,128]{2,0,1:T(8,128)(2,1)S(1)}, u32[]{:S(2)}, u32[]{:S(2)}) async-start(bf16[12,32,128]{2,0,1:T(8,128)(2,1)} %copy.33), calls=%async_computation.1 | async-start | bytes 262144 | tf_op jit(solution)/shard_map/all_to_all | solution.py:81
  176.5 0.3 fusion.83
  176.8 6.4 %all-to-all-done.1 = bf16[12,32,128]{2,0,1:T(8,128)(2,1)S(1)} async-done(((bf16[12,32,128]{2,0,1:T(8,128)(2,1)}), bf16[12,32,128]{2,0,1:T(8,128)(2,1)S(1)}, u32[]{:S(2)}, u32[]{:S(2)}) %all-to-all-start.1) | async-done | bytes 98336 | tf_op jit(solution)/shard_map/all_to_all | solution.py:81
  183.3 0.8 fusion.11
  (39 shorter events, 0.6 us)
Async XLA Ops:
  0.0 183.3 %copy-start = (bf16[3072,64]{0,1:T(8,128)(2,1)S(1)}, bf16[3072,64]{0,1:T(8,128)(2,1)}, u32[]{:S(2)}) copy-start(bf16[3072,64]{0,1:T(8,128)(2,1)} %param.12) | copy-start | bytes 1179652
  6.4 48.3 %copy-start.3 = (bf16[64,1000]{1,0:T(8,128)(2,1)S(1)}, bf16[64,1000]{1,0:T(8,128)(2,1)}, u32[]{:S(2)}) copy-start(bf16[64,1000]{1,0:T(8,128)(2,1)} %param.17) | copy-start | bytes 384004
  6.4 89.0 %copy-start.5 = (s32[4]{0:T(128)S(1)}, s32[4]{0:T(128)}, u32[]{:S(2)}) copy-start(s32[4]{0:T(128)} %param.18) | copy-start | bytes 52
  6.5 91.6 %copy-start.2 = (bf16[3,4,4,3072]{3,2,1,0:T(4,128)(2,1)S(1)}, bf16[3,4,4,3072]{3,2,1,0:T(4,128)(2,1)}, u32[]{:S(2)}) copy-start(bf16[3,4,4,3072]{3,2,1,0:T(4,128)(2,1)} %param.10) | copy-start | bytes 884740
  6.5 91.8 %copy-start.4 = (s32[3,4,4]{2,1,0:T(4,128)S(1)}, s32[3,4,4]{2,1,0:T(4,128)}, u32[]{:S(2)}) copy-start(s32[3,4,4]{2,1,0:T(4,128)} %param.11) | copy-start | bytes 580
  6.5 105.9 %copy-start.6 = (s32[4]{0:T(128)S(1)}, s32[4]{0:T(128)}, u32[]{:S(2)}) copy-start(s32[4]{0:T(128)} %param.19) | copy-start | bytes 52
  6.5 105.9 %copy-start.7 = (u32[32]{0:T(128)S(1)}, u32[32]{0:T(128)}, u32[]{:S(2)}) copy-start(u32[32]{0:T(128)} %constant.129) | copy-start | bytes 388
  95.7 3.9 %collective-permute-start = (f32[4,64]{1,0:T(4,128)S(1)}, f32[4,64]{1,0:T(4,128)S(1)}, u32[]{:S(2)}, u32[]{:S(2)}) collective-permute-start(f32[4,64]{1,0:T(4,128)S(1)} %fusion.77), channel_id=1, source_target_pairs={{0,1},{1,0},{2,3},{3,2},{4,5},{5,4},{6,7},{7,6},{8,9},{9,8},{10,11... | collective-permute-start | bytes 3080 | tf_op jit(solution)/shard_map/ppermute | solution.py:108
  99.6 3.6 %collective-permute-start.1 = (f32[4,128]{1,0:T(4,128)S(1)}, f32[4,128]{1,0:T(4,128)S(1)}, u32[]{:S(2)}, u32[]{:S(2)}) collective-permute-start(f32[4,128]{1,0:T(4,128)S(1)} %maximum_select_fusion.6), channel_id=1, source_target_pairs={{0,2},{1,3},{2,0},{3,1},{4,6},{5,7},{6,4},{7,5},{8,10},{9,11},{10,... | collective-permute-start | bytes 6152 | tf_op jit(solution)/shard_map/ppermute | solution.py:108
  103.3 1.2 collective-permute-start.2
  104.4 4.9 %collective-permute-start.3 = (f32[4,512]{1,0:T(4,128)S(1)}, f32[4,512]{1,0:T(4,128)S(1)}, u32[]{:S(2)}, u32[]{:S(2)}) collective-permute-start(f32[4,512]{1,0:T(4,128)S(1)} %maximum_select_fusion.2), channel_id=1, source_target_pairs={{0,8},{1,9},{2,10},{3,11},{4,12},{5,13},{6,14},{7,15},{8,0},{9,1},... | collective-permute-start | bytes 24584 | tf_op jit(solution)/shard_map/ppermute | solution.py:108
  105.8 46.6 %all-to-all-start = ((bf16[3,96,4,128]{3,2,0,1:T(4,128)(2,1)}), bf16[3,96,4,128]{3,2,0,1:T(4,128)(2,1)S(1)}, u32[]{:S(2)}, u32[]{:S(2)}) async-start(bf16[3,96,4,128]{3,2,0,1:T(4,128)(2,1)} %copy.28), calls=%async_computation | async-start | bytes 589824 | tf_op jit(solution)/shard_map/all_to_all | solution.py:52
  109.4 11.1 %collective-permute-start.4 = (f32[4,1024]{1,0:T(4,128)S(1)}, f32[4,1024]{1,0:T(4,128)S(1)}, u32[]{:S(2)}, u32[]{:S(2)}) collective-permute-start(f32[4,1024]{1,0:T(4,128)S(1)} %maximum_select_fusion.1), channel_id=1, source_target_pairs={{0,16},{1,17},{2,18},{3,19},{4,20},{5,21},{6,22},{7,23},{8,24},{9,... | collective-permute-start | bytes 49160 | tf_op jit(solution)/shard_map/ppermute | solution.py:108
  129.4 6.1 %copy-start.1 = (bf16[64,2048]{1,0:T(8,128)(2,1)S(1)}, bf16[64,2048]{1,0:T(8,128)(2,1)}, u32[]{:S(2)}) copy-start(bf16[64,2048]{1,0:T(8,128)(2,1)} %param.14) | copy-start | bytes 786436
  173.2 10.1 %all-to-all-start.1 = ((bf16[12,32,128]{2,0,1:T(8,128)(2,1)}), bf16[12,32,128]{2,0,1:T(8,128)(2,1)S(1)}, u32[]{:S(2)}, u32[]{:S(2)}) async-start(bf16[12,32,128]{2,0,1:T(8,128)(2,1)} %copy.33), calls=%async_computation.1 | async-start | bytes 262144 | tf_op jit(solution)/shard_map/all_to_all | solution.py:81
